TPU v7x, 32 devices: a whole 2x2x4 slice. The times are simulated.
32 devices in a mesh: seq: 8 (over z, x), tp: 4 (over y, core).
Axes of the slice: x: 2, y: 2, z: 4, core: 2. Of those that a mesh axis runs over, the one named last changes fastest.
Arguments:
- queries: bfloat16 [4096, 4096], P('seq', 'tp'), may hold values from -6 to 6
- keys: bfloat16 [4096, 4096], P('seq', 'tp'), may hold values from -6 to 6
- values: bfloat16 [4096, 4096], P('seq', 'tp'), may hold values from -6 to 6
- grad_out: bfloat16 [4096, 4096], P('seq', 'tp'), may hold values from -16 to 16
- out_weight: bfloat16 [4096, 4096], P('tp'), may hold values from -0.09375 to 0.09375
- norm_gain: float32 [4096], P('tp'), may hold values from 0.1 to 1.9
- doc_ids: int32 [4096], P('seq'), may hold values from 0 to 3, never falling along the last dimension, each value on 1 to 2048 neighbouring positions
Outputs:
- query_grad: bfloat16 [4096, 4096], P('seq', 'tp')
- key_grad: bfloat16 [4096, 4096], P('seq', 'tp')
- value_grad: bfloat16 [4096, 4096], P('seq', 'tp')
- out_proj_grad: float32 [4096, 4096], P('seq', 'tp')
Inputs may be any that keep to these rules, and one draw needn't show every extreme that they name: `doc_ids`: document ids never fall along the sequence; each document has 1 to 2048 positions and one has exactly 2048.
All inputs are finite; a program needn't handle non-finite values.
Results may differ from a plain program's by a relative error of at most 0.012.
Values may be sent and summed in bfloat16 or wider, within the bound.
A program may use at most 128 MiB of HBM per device.

v0:
```python
import math

import jax
import jax.numpy as jnp
from jax import lax
from jax.sharding import PartitionSpec as P

HEAD_DIM = 128


EPS = 1e-06


def feature(x):
    return jnp.where(x > 0, x + 1.0, jnp.exp(jnp.minimum(x, 0.0)))


def feature_slope(x):
    return jnp.where(x > 0, 1.0, jnp.exp(jnp.minimum(x, 0.0)))


def combine(earlier, later):
    state_early, tag_early = earlier
    state_late, tag_late = later
    vacant = tag_late < 0
    joined = state_late + jnp.where(tag_early == tag_late, state_early, 0.0)
    return (jnp.where(vacant, state_early, joined), jnp.where(vacant, tag_early, tag_late))


def local(queries, keys, values, grad_out, out_weight, norm_gain, doc_ids):
    tok_rows, feat_width = queries.shape
    head_count = feat_width // HEAD_DIM
    block_rows = min(512, tok_rows)
    block_count = tok_rows // block_rows
    feat_q = feature(queries.astype(jnp.float32)).astype(jnp.bfloat16)
    feat_k = feature(keys.astype(jnp.float32)).astype(jnp.bfloat16)
    whole = lax.all_gather(grad_out, "tp", axis=1, tiled=True)
    upstream = lax.dot_general(
        whole, out_weight, (((1,), (1,)), ((), ())), preferred_element_type=jnp.float32
    )
    doc_float = doc_ids.astype(jnp.float32)
    gain = norm_gain.reshape(head_count, HEAD_DIM)
    positions = jnp.arange(block_rows)
    causal = positions[:, None] >= positions[None, :]
    empty_state = jnp.zeros((head_count, HEAD_DIM, HEAD_DIM), jnp.float32)
    identity = (empty_state, jnp.full((1,), -1.0, jnp.float32))
    my_index = lax.axis_index("seq")

    def cut(array):
        return array.reshape(block_rows, head_count, HEAD_DIM)

    def doc_rows():
        return doc_float

    def pair_weights(query_block, key_block, doc_block):
        allowed = causal & (doc_block[:, None] == doc_block[None, :])
        scores = jnp.einsum(
            "thd,shd->hts", query_block, key_block, preferred_element_type=jnp.float32
        )
        return (jnp.where(allowed[None], scores, 0.0).astype(jnp.bfloat16), allowed)

    doc_block = doc_rows()
    last_doc = doc_block[-1:]
    key_block = cut(feat_k)
    chosen = (doc_block == last_doc)[:, None, None]
    picked = jnp.where(chosen, key_block, jnp.zeros_like(key_block))
    summary = jnp.einsum("shd,she->hde", picked, cut(values), preferred_element_type=jnp.float32)
    forward_parts = (summary, last_doc)
    local_total = identity
    local_total = combine(local_total, forward_parts)
    first_doc = doc_float[0:1]
    pieces = lax.all_gather(local_total[0][None], "seq", axis=0, tiled=True)
    piece_tags = lax.all_gather(local_total[1], "seq", axis=0, tiled=True)
    owners = jnp.arange(piece_tags.shape[0], dtype=jnp.int32)
    taken = (owners < my_index) & (piece_tags == first_doc[0])
    prior = jnp.sum(jnp.where(taken[:, None, None, None], pieces, 0.0), axis=0)
    carry = (prior, first_doc)
    query_block = cut(feat_q)
    doc_block = doc_rows()
    weight, allowed = pair_weights(query_block, cut(feat_k), doc_block)
    inner = jnp.einsum("hts,she->the", weight, cut(values), preferred_element_type=jnp.float32)
    outer = jnp.einsum(
        "thd,hde->the",
        query_block,
        carry[0].astype(jnp.bfloat16),
        preferred_element_type=jnp.float32,
    )
    outputs = inner + jnp.where((doc_block == carry[1])[:, None, None], outer, 0.0)
    states_in = [carry]
    inv_rms = lax.rsqrt(jnp.mean(outputs * outputs, axis=-1, keepdims=True) + EPS)
    normed = (outputs * inv_rms * gain).astype(jnp.bfloat16)
    scaled = upstream.reshape(tok_rows, head_count, HEAD_DIM) * gain
    grad_attn = (
        scaled * inv_rms - outputs * inv_rms**3 * jnp.mean(outputs * scaled, axis=-1, keepdims=True)
    ).astype(jnp.bfloat16)
    normed_rows = normed.reshape(tok_rows, feat_width)
    grad_rows = grad_attn.reshape(tok_rows, feat_width)
    seq_count = lax.axis_size("seq")
    factor = 1.0 / math.sqrt(tok_rows * seq_count)
    which = 0
    doc_block = doc_rows()
    first_doc = doc_block[0:1]
    query_block = cut(feat_q)
    chosen = (doc_block == first_doc)[:, None, None]
    picked = jnp.where(chosen, query_block, jnp.zeros_like(query_block))
    summary = jnp.einsum("thd,the->hde", picked, cut(grad_rows), preferred_element_type=jnp.float32)
    reverse_parts = [(summary, first_doc)]
    local_back = identity
    for which in reversed(range(block_count)):
        local_back = combine(local_back, reverse_parts[which])
    last_doc = doc_float[-1:]
    pieces = lax.all_gather(local_back[0][None], "seq", axis=0, tiled=True)
    piece_tags = lax.all_gather(local_back[1], "seq", axis=0, tiled=True)
    owners = jnp.arange(piece_tags.shape[0], dtype=jnp.int32)
    taken = (owners > my_index) & (piece_tags == last_doc[0])
    later = jnp.sum(jnp.where(taken[:, None, None, None], pieces, 0.0), axis=0)
    back = (later, last_doc)
    query_list = []
    key_list = []
    value_list = []
    for which in reversed(range(block_count)):
        query_block = cut(feat_q)
        key_block = cut(feat_k)
        value_block = cut(values)
        grad_block = cut(grad_rows)
        doc_block = doc_rows()
        state, tag = states_in[which]
        weight, allowed = pair_weights(query_block, key_block, doc_block)
        dot_grad = jnp.einsum(
            "the,she->hts", grad_block, value_block, preferred_element_type=jnp.float32
        )
        grad_weight = jnp.where(allowed[None], dot_grad, 0.0).astype(jnp.bfloat16)
        dround = back[0].astype(jnp.bfloat16)
        sround = state.astype(jnp.bfloat16)
        later_rows = (doc_block == back[1])[:, None, None]
        earlier_rows = (doc_block == tag)[:, None, None]
        value_part = jnp.einsum(
            "hts,the->she", weight, grad_block, preferred_element_type=jnp.float32
        )
        value_part = value_part + jnp.where(
            later_rows,
            jnp.einsum("shd,hde->she", key_block, dround, preferred_element_type=jnp.float32),
            0.0,
        )
        key_part = jnp.einsum(
            "hts,thd->shd", grad_weight, query_block, preferred_element_type=jnp.float32
        )
        key_part = key_part + jnp.where(
            later_rows,
            jnp.einsum("she,hde->shd", value_block, dround, preferred_element_type=jnp.float32),
            0.0,
        )
        query_part = jnp.einsum(
            "hts,shd->thd", grad_weight, key_block, preferred_element_type=jnp.float32
        )
        query_part = query_part + jnp.where(
            earlier_rows,
            jnp.einsum("the,hde->thd", grad_block, sround, preferred_element_type=jnp.float32),
            0.0,
        )
        query_list.append(
            (query_part * feature_slope(cut(queries).astype(jnp.float32))).astype(jnp.bfloat16)
        )
        key_list.append(
            (key_part * feature_slope(cut(keys).astype(jnp.float32))).astype(jnp.bfloat16)
        )
        value_list.append(value_part.astype(jnp.bfloat16))
        back = combine(back, reverse_parts[which])
    shape = (tok_rows, feat_width)
    query_grad = jnp.concatenate(query_list[::-1], axis=0).reshape(shape)
    key_grad = jnp.concatenate(key_list[::-1], axis=0).reshape(shape)
    value_grad = jnp.concatenate(value_list[::-1], axis=0).reshape(shape)
    weight_grad = lax.psum_scatter(
        (
            lax.dot_general(
                whole, normed_rows, (((0,), (0,)), ((), ())), preferred_element_type=jnp.float32
            )
            * factor
        ).astype(jnp.bfloat16),
        "seq",
        scatter_dimension=0,
        tiled=True,
    ).astype(jnp.float32)
    return (query_grad, key_grad, value_grad, weight_grad)


def solution(mesh):
    in_specs = (
        P("seq", "tp"),
        P("seq", "tp"),
        P("seq", "tp"),
        P("seq", "tp"),
        P("tp", None),
        P("tp"),
        P("seq"),
    )
    out_specs = (P("seq", "tp"), P("seq", "tp"), P("seq", "tp"), P("seq", "tp"))
    return jax.shard_map(local, mesh=mesh, in_specs=in_specs, out_specs=out_specs, check_vma=False)
```

profile of v0, /device:TPU:0, one launch (start us, length us, event | category | flops | bytes accessed | tf_op | source)
XLA Modules:
  0.0 360.2 jit_solution(16338589126438625096)
XLA Ops:
  7.2 0.7 all-gather.6.cloned.1.call-update
  8.0 0.7 convert_element_type.62
  8.7 3.2 fusion.4
  11.9 1.3 copy.68
  13.2 1.6 copy.45
  14.9 0.7 dynamic-slice
  15.5 1.3 select_dynamic-update-slice_fusion
  17.4 1.2 broadcast_compare_fusion
  18.6 1.2 convolution_select_fusion.1
  19.9 0.0 all-gather.10.cloned.1.call-start
  20.0 0.8 select_dynamic-update-slice_fusion.1
  20.8 23.3 %all-reduce.2 = (f32[8]{0:T(128)S(1)}, f32[8]{0:T(128)S(1)}) all-reduce(f32[8]{0:T(128)S(1)} %select_dynamic-update-slice_fusion.1, f32[8]{0:T(128)S(1)} %get-tuple-element.25), channel_id=1, replica_groups=mesh['seq'=8,'tp'=4] {'seq'}, use_global_device_ids=true, to_apply=%add | all-reduce | flops 16 | bytes 128
  44.8 3.5 fusion.6
  48.2 1.5 copy.65
  49.7 0.7 compare_and_fusion.1
  50.4 0.2 fusion.20
  50.7 1.4 select_convert_fusion.1
  52.1 1.9 copy-done.1
  54.0 2.9 fusion.11
  56.9 10.8 %fusion.39 = f32[512,1024]{0,1:T(8,128)} fusion(bf16[512,4096]{1,0:T(8,128)(2,1)} %all-gather.6.cloned.1.call-done, bf16[1024,4096]{1,0:T(8,128)(2,1)} %param.11), kind=kOutput, calls=%fused_computation.70 | convolution fusion | flops 4294967296 | bytes 14680064 | tf_op jit(solution)/shard_map/reshape | solution.py:92
  67.7 54.6 %all-gather.8.cloned.1.call-done = f32[64,128,128]{2,1,0:T(8,128)} async-done(((f32[8,128,128]{2,1,0:T(8,128)}), f32[64,128,128]{2,1,0:T(8,128)}) %all-gather.8.cloned.1.call-update) | async-done | bytes 4194320 | tf_op jit(solution)/shard_map/all_gather | solution.py:72
  122.3 2.9 select_reduce_fusion.1
  125.2 0.6 copy-done.7
  125.8 0.9 multiply_reduce_fusion.1
  126.7 1.7 multiply_convert_fusion.1
  128.4 1.2 convolution_select_fusion
  129.6 0.3 reduce-scatter.2.cloned.1.call-start
  129.9 10.3 %fusion = bf16[4096,1024]{0,1:T(8,128)(2,1)} fusion(bf16[512,1024]{0,1:T(8,128)(2,1)} %bitcast.98, bf16[512,4096]{1,0:T(8,128)(2,1)} %all-gather.6.cloned.1.call-done), kind=kOutput, calls=%fused_computation.3 | convolution fusion | flops 4303355904 | bytes 13631488 | tf_op jit(solution)/shard_map/dot_general | solution.py:175
  140.2 3.0 copy.47
  143.2 2.9 copy.52
  146.0 0.5 compare_and_fusion
  146.6 2.4 select_convert_fusion
  149.1 1.5 fusion.40
  150.6 0.6 copy-done.2
  151.2 1.0 copy-done.8
  152.2 1.4 fusion.10
  153.6 2.3 copy.55
  155.9 4.4 %fusion.42 = f32[8,128,512]{2,1,0:T(8,128)} fusion(bf16[512,8,128]{0,2,1:T(8,128)(2,1)S(1)} %get-tuple-element.17, bf16[8,512,512]{2,1,0:T(8,128)(2,1)} %copy-done.1), kind=kOutput, calls=%fused_computation.73 | convolution fusion | flops 536870912 | bytes 7340032 | tf_op jit(solution)/shard_map/hts,the->she/dot_general | solution.py:137
  160.3 2.1 fusion.41
  162.4 38.7 %all-gather.10.cloned.1.call-done = f32[64,128,128]{2,1,0:T(8,128)} async-done(((f32[8,128,128]{2,1,0:T(8,128)}), f32[64,128,128]{2,1,0:T(8,128)}) %all-gather.10.cloned.1.call-update) | async-done | bytes 4194320 | tf_op jit(solution)/shard_map/all_gather | solution.py:112
  201.1 2.9 select_reduce_fusion
  204.0 0.2 copy-done.10
  204.2 1.5 add_convert_fusion
  205.7 2.4 copy.57
  208.1 3.1 fusion.9
  211.3 2.3 copy.56
  213.5 137.5 %reduce-scatter.2.cloned.1.call-done = bf16[512,1024]{0,1:T(8,128)(2,1)} async-done(((bf16[4096,1024]{0,1:T(8,128)(2,1)}), bf16[512,1024]{0,1:T(8,128)(2,1)}) %reduce-scatter.2.cloned.1.call-update) | async-done | bytes 1048592 | tf_op jit(solution)/shard_map/reduce_scatter | solution.py:173
  351.1 2.6 copy.58
  (38 shorter events, 0.2 us)
Async XLA Ops:
  7.2 11.4 %copy-start = (bf16[512,1024]{1,0:T(8,128)(2,1)S(1)}, bf16[512,1024]{1,0:T(8,128)(2,1)}, u32[]{:S(2)}) copy-start(bf16[512,1024]{1,0:T(8,128)(2,1)} %param.9) | copy-start | bytes 3145732
  7.2 49.7 %all-gather.6.cloned.1.call-start = ((), (), s32[]{:S(2)}) async-start(), calls=%async_computation.1 | async-start | bytes 5242880 | tf_op jit(solution)/shard_map/all_gather | solution.py:37
  7.9 114.4 %all-gather.8.cloned.1.call-start = ((), (), s32[]{:S(2)}) async-start(), calls=%async_computation.3 | async-start | bytes 4718592 | tf_op jit(solution)/shard_map/all_gather | solution.py:72
  11.9 38.8 %copy-start.9 = (bf16[64,8,8,128]{3,2,1,0:T(8,128)(2,1)}, bf16[64,8,8,128]{3,2,1,0:T(8,128)(2,1)S(1)}, u32[]{:S(2)}) copy-start(bf16[64,8,8,128]{3,2,1,0:T(8,128)(2,1)S(1)} %get-tuple-element.19) | copy-start | bytes 3145732
  11.9 3.0 copy-start.16
  11.9 5.5 %copy-start.15 = (s32[512]{0:T(512)S(1)}, s32[512]{0:T(512)}, u32[]{:S(2)}) copy-start(s32[512]{0:T(512)} %param.13) | copy-start | bytes 6148
  14.8 5.1 %copy-start.11 = (bf16[512,8,128]{0,2,1:T(8,128)(2,1)}, bf16[512,8,128]{0,2,1:T(8,128)(2,1)S(1)}, u32[]{:S(2)}) copy-start(bf16[512,8,128]{0,2,1:T(8,128)(2,1)S(1)} %copy.45) | copy-start | bytes 3145732
  19.9 181.2 %all-gather.10.cloned.1.call-start = ((), (), s32[]{:S(2)}) async-start(), calls=%async_computation.4 | async-start | bytes 4718592 | tf_op jit(solution)/shard_map/all_gather | solution.py:112
  50.7 1.4 copy-start.13
  52.1 1.9 copy-start.1
  122.3 2.9 copy-start.4
  122.3 3.5 copy-start.7
  122.3 3.5 copy-start.14
  129.6 221.4 %reduce-scatter.2.cloned.1.call-start = ((), (), s32[]{:S(2)}) async-start(), calls=%async_computation.2 | async-start | bytes 9437184 | tf_op jit(solution)/shard_map/reduce_scatter | solution.py:173
  146.6 2.5 copy-start.12
  149.1 2.1 copy-start.2
  149.1 3.1 copy-start.8
  155.9 4.4 %copy-start.3 = (bf16[8,512,512]{2,1,0:T(8,128)(2,1)S(1)}, bf16[8,512,512]{2,1,0:T(8,128)(2,1)}, u32[]{:S(2)}) copy-start(bf16[8,512,512]{2,1,0:T(8,128)(2,1)} %copy-done.2) | copy-start | bytes 12582916
  201.1 2.9 copy-start.6
  201.1 3.1 copy-start.10
  205.7 2.4 copy-start.5
Sparse Core Ops, SparseCore 0:
  9.5 37.1 all-gather.5
  49.5 72.7 all-gather.7
  129.8 71.2 all-gather.9
  204.6 146.4 reduce-scatter.1
where the time goes:
time: 361 us; the launch traced here: 360 us
  waiting for transfers between devices  232 us (64%)
  matrix products  45.2 us (13%)
  local copies, waits for them, and re-layouts  24.9 us (7%)
  blocking collectives  23.3 us (6%)
  other arithmetic  19.6 us (5%)
  between operations  15.3 us (4%)
    reduce_scatter x1, waiting for transfers between devices, local(): lax.psum_scatter((lax.dot_general(whole, normed_rows, (((0,), (0,)), ((),...  138 us
    all_gather x1, waiting for transfers between devices, local(): pieces = lax.all_gather(local_total[0][None], 'seq', axis=0, tiled=True)  54.6 us
    all_gather x1, waiting for transfers between devices, local(): pieces = lax.all_gather(local_back[0][None], 'seq', axis=0, tiled=True)  38.7 us
    unnamed x1, blocking collectives  23.3 us
    unnamed x42, local copies, waits for them, and re-layouts  16 us
    reshape x1, matrix products, local(): scaled = upstream.reshape(tok_rows, head_count, HEAD_DIM) * gain  10.8 us
    dot_general x1, matrix products, local(): lax.dot_general(whole, normed_rows, (((0,), (0,)), ((), ())), preferred_e...  10.3 us
  transfers between devices with their start and end apart: 4, of which 3 were waited for; matrix products, arithmetic and copies ran while one was open for 21% of the time, Pallas kernels for 0%

commit v1 on v0

v1 whole, which is shorter than its diff:
```python
import functools
import math

import jax
import jax.numpy as jnp
from jax import lax
from jax.experimental import pallas as pl
from jax.experimental.pallas import tpu as pltpu
from jax.sharding import PartitionSpec as P

HEAD = 128
EPS = 1e-06
PAD = 16
BF = jnp.bfloat16
F32 = jnp.float32


def feature(x):
    return jnp.where(x > 0, x + 1.0, jnp.exp(jnp.minimum(x, 0.0)))


def slope(x):
    return jnp.where(x > 0, 1.0, jnp.exp(jnp.minimum(x, 0.0)))


def dot(a, b, ca, cb):
    return lax.dot_general(a, b, (((ca,), (cb,)), ((), ())), preferred_element_type=F32)


def causal_mask(col, row):
    rows = col.shape[0]
    at = lax.broadcasted_iota(jnp.int32, (rows, rows), 0)
    to = lax.broadcasted_iota(jnp.int32, (rows, rows), 1)
    return (at >= to) & (col == row)


MESH = pl.DeviceIdType.MESH


def layer_kernel(
    dims, q_ref, k_ref, v_ref, go_hbm, w_hbm, gain_ref, col_ref, row_ref,
    oq_ref, ok_ref, ov_ref, ow_ref,
    whole, theirs, w_ref, attn_ref, pair, grad_ref, state, own, oth, ein, eout,
    acc, sent, got, lsem, tsem, xsem, psem, osem, esem, rsem,
):
    n, tp, depth, mrows, width, parts, factor = dims
    rows, feats = q_ref.shape
    heads = feats // HEAD
    hc = 2
    chunks = heads // hc
    body = hc * HEAD
    each = feats // parts
    me = lax.axis_index("seq")
    j = lax.axis_index("tp")
    x = me % 2
    z = me // 2
    mate = me + 1 - 2 * x
    bits = tp.bit_length() - 1
    last = depth - 1
    mine_at = pl.ds(pl.multiple_of(x * mrows, mrows), mrows)
    mate_at = pl.ds(pl.multiple_of((1 - x) * mrows, mrows), mrows)

    def rc(src, dst, sems, at, dev):
        return pltpu.make_async_remote_copy(
            src_ref=src, dst_ref=dst, send_sem=sems.at[0, at], recv_sem=sems.at[1, at],
            device_id=dev, device_id_type=MESH,
        )

    def peer(b):
        bit = 1 << b
        return {"tp": j + bit * (1 - 2 * ((j // bit) % 2))}

    load_go = pltpu.make_async_copy(go_hbm, whole.at[0], lsem.at[0])
    load_w = pltpu.make_async_copy(w_hbm, w_ref, lsem.at[1])
    load_go.start()
    load_w.start()

    barrier = pltpu.get_barrier_semaphore()
    fixed = [{"seq": mate}] + [peer(b) for b in range(bits)]
    for dev in fixed:
        pl.semaphore_signal(barrier, inc=1, device_id=dev, device_id_type=MESH)

    @pl.when(z > 0)
    def _():
        pl.semaphore_signal(barrier, inc=1, device_id={"seq": me - 2}, device_id_type=MESH)

    @pl.when(z < last)
    def _():
        pl.semaphore_signal(barrier, inc=1, device_id={"seq": me + 2}, device_id_type=MESH)

    sides = (z + depth - 1) // depth + (last - z + depth - 1) // depth
    pl.semaphore_wait(barrier, len(fixed) + sides)

    def piece(buf, off, k, b):
        return rc(buf.at[k], buf.at[k | (1 << b)], tsem, off + (k | (1 << b)), peer(b))

    def forward(buf, off, k):
        low = bits if k == 0 else (k & -k).bit_length() - 1
        for b in reversed(range(low)):
            piece(buf, off, k, b).start()

    def arrived(buf, off, k):
        b = (k & -k).bit_length() - 1
        piece(buf, off, k ^ (1 << b), b).wait_recv()

    load_go.wait()
    swap = rc(whole.at[0, :, mate_at], theirs.at[0], tsem, 0, {"seq": mate})
    col = col_ref[...]
    first = col[0:1, :]
    final = col[rows - 1 : rows, :]

    forward(whole, 0, 0)

    def relay(buf, off, upto):
        for k in range(1, tp):
            if ((k & -k) > 1) == upto:
                arrived(buf, off, k)
                forward(buf, off, k)

    def swap_copy(w, c):
        return rc(own.at[w, c], oth.at[w, c], osem, w * chunks + c, {"seq": mate})

    def carry_copy(w, c):
        return rc(eout.at[w, c], ein.at[w, c], esem, w * chunks + c, {"seq": lax.rem(me + 2 - 4 * w + n, n)})

    def put(w, c, left, right_at, edge):
        for i in range(hc):
            own[w, c, i * HEAD : (i + 1) * HEAD, :] = dot(left[i], right_at[i], 0, 0).astype(BF)
        own[w, c, body:, :] = jnp.broadcast_to(edge, (PAD, HEAD)).astype(BF)
        swap_copy(w, c).start()

    def carry_on(w, c):
        begins = (z == 0) if w == 0 else (z == last)
        ends = (z == last) if w == 0 else (z == 0)
        edge = first if w == 0 else final
        swap_copy(w, c).wait_recv()

        @pl.when(begins)
        def _():
            ein[w, c] = jnp.zeros(ein.shape[2:], BF)

        @pl.when(jnp.logical_not(begins))
        def _():
            carry_copy(w, c).wait_recv()

        def tag(ref):
            return ref[w, c, body : body + 1, :].astype(F32)

        a = own[w, c, :body, :].astype(F32)
        b = oth[w, c, :body, :].astype(F32)
        e = ein[w, c, :body, :].astype(F32)
        ta, tb, te = tag(own), tag(oth), tag(ein)
        front = x == w

        @pl.when(jnp.logical_not(ends))
        def _():
            late_tag = jnp.where(front, tb, ta)
            same = jnp.where(ta == tb, 1.0, 0.0)
            keep_a = jnp.where(front, same, 1.0)
            keep_b = jnp.where(front, 1.0, same)
            keep_e = jnp.where(te == late_tag, 1.0, 0.0)
            eout[w, c, :body, :] = (a * keep_a + b * keep_b + e * keep_e).astype(BF)
            eout[w, c, body:, :] = jnp.broadcast_to(late_tag, (PAD, HEAD)).astype(BF)
            carry_copy(w, c).start()

        near = jnp.where(front, 0.0, jnp.where(tb == edge, 1.0, 0.0))
        far = jnp.where(te == edge, 1.0, 0.0)
        state[w, c * body : (c + 1) * body, :] = (b * near + e * far).astype(BF)

    for c in range(chunks):
        ats = [slice((c * hc + i) * HEAD, (c * hc + i + 1) * HEAD) for i in range(hc)]
        picked = [
            jnp.where(col == final, feature(k_ref[:, at].astype(F32)), 0.0).astype(BF) for at in ats
        ]
        put(0, c, picked, [v_ref[:, at] for at in ats], final)
    swap.start()
    for c in range(chunks):
        carry_on(0, c)
    swap.wait_recv()
    forward(theirs, tp, 0)

    def pair_copy(c):
        return rc(pair.at[c, 0], pair.at[c, 1], psem, c, {"seq": mate})

    per = each // HEAD
    for c in range(parts):

        @pl.loop(0, per)
        def _(i):
            at = pl.ds(pl.multiple_of(c * each + i * HEAD, HEAD), HEAD)
            to = pl.ds(pl.multiple_of(i * HEAD, HEAD), HEAD)
            fq = feature(q_ref[:, at].astype(F32)).astype(BF)
            fk = feature(k_ref[:, at].astype(F32)).astype(BF)
            mask = causal_mask(col, row_ref[...])
            weight = jnp.where(mask, dot(fq, fk, 1, 1), 0.0).astype(BF)
            attn = dot(weight, v_ref[:, at], 1, 0)
            attn = attn + jnp.where(col == first, dot(fq, state[0, at, :], 1, 0), 0.0)
            inv = lax.rsqrt(jnp.mean(attn * attn, axis=-1, keepdims=True) + EPS)
            attn_ref[:, at] = attn
            pair[c, 0, :, to] = (attn * inv * gain_ref[:, at]).astype(BF)

        pair_copy(c).start()
    relay(whole, 0, True)
    relay(theirs, tp, True)
    relay(whole, 0, False)
    relay(theirs, tp, False)

    def partial(c, dest):
        k = jnp.int32(0)
        for b in range(bits):
            k = k + (1 << b) * ((dest // (1 << b) + j // (1 << b)) % 2)
        value = dot(whole[k, :, mine_at], pair[c, 0], 0, 0) + dot(theirs[k], pair[c, 1], 0, 0)
        return value * factor

    def chain(w, c, t):
        at = (w * parts + c) * last + t
        return rc(
            sent.at[w, c, t], got.at[w, c, t], rsem, at, {"seq": lax.rem(me + 2 - 4 * w + n, n)}
        )

    def on_way(w, t):
        return (z <= t) if w == 0 else (z >= last - t)

    def send_step(w, c, t):
        @pl.when(on_way(w, t))
        def _():
            dest = last - t + z if w == 0 else z - last + t
            acc[...] = partial(c, dest)
            if t > 0:

                @pl.when((z > 0) if w == 0 else (z < last))
                def _():
                    chain(w, c, t - 1).wait_recv()
                    acc[...] += got[w, c, t - 1].astype(F32)

            sent[w, c, t] = acc[...].astype(BF)
            chain(w, c, t).start()

    for c in range(parts):
        pair_copy(c).wait_recv()
        for w in range(2):
            send_step(w, c, 0)

    load_w.wait()
    for c in range(chunks):
        at = slice(c * body, (c + 1) * body)
        total = None
        for k in range(tp):
            owner = jnp.int32(0)
            for b in range(bits):
                owner = owner + (1 << b) * (((k >> b) + j // (1 << b)) % 2)
            start = pl.multiple_of(owner * width, width)
            term = dot(whole[k], w_ref[at, pl.ds(start, width)], 1, 1)
            total = term if total is None else total + term
        left, right = [], []
        for i in range(hc):
            cut = slice(c * body + i * HEAD, c * body + (i + 1) * HEAD)
            attn = attn_ref[:, cut]
            inv = lax.rsqrt(jnp.mean(attn * attn, axis=-1, keepdims=True) + EPS)
            scaled = total[:, i * HEAD : (i + 1) * HEAD] * gain_ref[:, cut]
            mean = jnp.mean(attn * scaled, axis=-1, keepdims=True)
            grad = (scaled * inv - attn * (inv * inv * inv) * mean).astype(BF)
            grad_ref[:, cut] = grad
            left.append(jnp.where(col == first, feature(q_ref[:, cut].astype(F32)), 0.0).astype(BF))
            right.append(grad)
        put(1, c, left, right, first)

    def grads(begin, end):
        @pl.loop(begin, end)
        def _(h):
            at = pl.ds(pl.multiple_of(h * HEAD, HEAD), HEAD)
            mask = causal_mask(col, row_ref[...])
            q = q_ref[:, at].astype(F32)
            k = k_ref[:, at].astype(F32)
            v = v_ref[:, at]
            g = grad_ref[:, at]
            fq = feature(q).astype(BF)
            fk = feature(k).astype(BF)
            weight = jnp.where(mask, dot(fq, fk, 1, 1), 0.0).astype(BF)
            gw = jnp.where(mask, dot(g, v, 1, 1), 0.0).astype(BF)
            early = col == first
            late = col == final
            s = state[0, at, :]
            d = state[1, at, :]
            vp = dot(weight, g, 0, 0) + jnp.where(late, dot(fk, d, 1, 0), 0.0)
            ov_ref[:, at] = vp.astype(BF)
            kp = dot(gw, fq, 0, 0) + jnp.where(late, dot(v, d, 1, 1), 0.0)
            ok_ref[:, at] = (kp * slope(k)).astype(BF)
            qp = dot(gw, fk, 1, 0) + jnp.where(early, dot(g, s, 1, 1), 0.0)
            oq_ref[:, at] = (qp * slope(q)).astype(BF)

    def steps(t):
        for c in range(parts):
            for w in range(2):
                send_step(w, c, t)

    for t in range(1, min(2, last)):
        steps(t)
    for c in range(chunks):
        carry_on(1, c)
    grads(0, heads // 2)
    for t in range(2, last):
        steps(t)
    grads(heads // 2, heads)
    for c in range(parts):
        ow_ref[:, c * each : (c + 1) * each] = partial(c, z)
    for c in range(parts):
        for w in range(2):

            @pl.when((z > 0) if w == 0 else (z < last))
            def _():
                chain(w, c, last - 1).wait_recv()
                ow_ref[:, c * each : (c + 1) * each] += got[w, c, last - 1].astype(F32)

    swap.wait_send()
    for buf, off in ((whole, 0), (theirs, tp)):
        for k in range(1, tp):
            b = (k & -k).bit_length() - 1
            piece(buf, off, k ^ (1 << b), b).wait_send()
    for c in range(parts):
        pair_copy(c).wait_send()
    for w in range(2):
        for c in range(chunks):
            swap_copy(w, c).wait_send()

            @pl.when((z < last) if w == 0 else (z > 0))
            def _():
                carry_copy(w, c).wait_send()

        for c in range(parts):
            for t in range(last):

                @pl.when(on_way(w, t))
                def _():
                    chain(w, c, t).wait_send()


def local(queries, keys, values, grad_out, out_weight, norm_gain, doc_ids):
    rows, feats = queries.shape
    n = lax.axis_size("seq")
    tp = lax.axis_size("tp")
    depth = n // 2
    model = out_weight.shape[1]
    width = model // tp
    mrows = model // n
    parts = 2
    each = feats // parts
    heads = feats // HEAD
    chunks = heads // 2
    last = depth - 1
    docs = doc_ids.astype(F32)
    dims = (n, tp, depth, mrows, width, parts, 1.0 / math.sqrt(rows * n))
    vmem = pl.BlockSpec(memory_space=pltpu.VMEM)
    anyspace = pl.BlockSpec(memory_space=pl.ANY)
    wide = jax.ShapeDtypeStruct((rows, feats), BF)
    summed = pltpu.VMEM((2, chunks, 2 * HEAD + PAD, HEAD), BF)
    sem = pltpu.SemaphoreType.DMA
    flops = 2 * rows * model * feats * 3
    return pl.pallas_call(
        functools.partial(layer_kernel, dims),
        in_specs=[vmem] * 3 + [anyspace] * 2 + [vmem] * 3,
        out_specs=[vmem] * 4,
        out_shape=[wide] * 3 + [jax.ShapeDtypeStruct((mrows, feats), F32)],
        scratch_shapes=[
            pltpu.VMEM((tp, rows, width), BF),
            pltpu.VMEM((tp, rows, mrows), BF),
            pltpu.VMEM((feats, model), BF),
            pltpu.VMEM((rows, feats), F32),
            pltpu.VMEM((parts, 2, rows, each), BF),
            pltpu.VMEM((rows, feats), BF),
            pltpu.VMEM((2, feats, HEAD), BF),
            summed, summed, summed, summed,
            pltpu.VMEM((mrows, each), F32),
            pltpu.VMEM((2, parts, last, mrows, each), BF),
            pltpu.VMEM((2, parts, last, mrows, each), BF),
            sem((2,)),
            sem((2, 2 * tp)),
            sem((2, 1)),
            sem((2, parts)),
            sem((2, 2 * chunks)),
            sem((2, 2 * chunks)),
            sem((2, 2 * parts * last)),
        ],
        compiler_params=pltpu.CompilerParams(
            collective_id=0, has_side_effects=True, vmem_limit_bytes=60 * 1024 * 1024
        ),
        cost_estimate=pl.CostEstimate(flops=flops, bytes_accessed=flops // 512, transcendentals=0),
        name="layer",
    )(queries, keys, values, grad_out, out_weight, norm_gain[None, :], docs[:, None], docs[None, :])


def solution(mesh):
    wide = P("seq", "tp")
    in_specs = (wide, wide, wide, wide, P("tp", None), P("tp"), P("seq"))
    return jax.shard_map(
        local, mesh=mesh, in_specs=in_specs, out_specs=(wide,) * 4, check_vma=False
    )
```

time: 361 us -> 143 us (0.40)
  waiting for transfers between devices: 232 us -> 0 us
  Pallas kernels: 0 us -> 135 us
  matrix products: 45.2 us -> 0 us
  blocking collectives: 23.3 us -> 0 us
  other arithmetic: 19.6 us -> 0.68 us
  local copies, waits for them, and re-layouts: 24.9 us -> 6.61 us
  between operations: 15.3 us -> 0.66 us
    reduce_scatter x1 -> x0, waiting for transfers between devices: 138 us -> none  [local(): lax.psum_scatter((lax.dot_general(whole, normed_rows, (((0,), (0,)), ((),...]
    pallas_call x0 -> x1, Pallas kernels: none -> 135 us  [local(): pl.pallas_call(functools.partial(layer_kernel, dims), in_specs=[vmem] * 3...]
    all_gather x3 -> x0, waiting for transfers between devices: 93.3 us -> none  [the longest x1 54.6 us: local(): pieces = lax.all_gather(local_total[0][None], 'seq', axis=0, tiled=True)]
    dot_general x13 -> x0, matrix products: 34.4 us -> none  [the longest x1 10.3 us: local(): lax.dot_general(whole, normed_rows, (((0,), (0,)), ((), ())), preferred_e...]
    unnamed x1 -> x0, blocking collectives: 23.3 us -> none
    reshape x1 -> x0, matrix products: 10.8 us -> none  [local(): scaled = upstream.reshape(tok_rows, head_count, HEAD_DIM) * gain]
    unnamed x42 -> x12, local copies, waits for them, and re-layouts: 16 us -> 5.75 us
    select_n x2 -> x0, local copies, waits for them, and re-layouts: 5.84 us -> none  [feature_slope(): return jnp.where(x > 0, 1.0, jnp.exp(jnp.minimum(x, 0.0)))]
  transfers between devices with their start and end apart: 4 -> 0, of which waited for: 3 -> 0; matrix products, arithmetic and copies ran while one was open for 21% -> 0% of each run, Pallas kernels for 0% -> 0%
where the time goes in v1:
time: 143 us
  Pallas kernels  135 us (94%)
  local copies, waits for them, and re-layouts  6.61 us (5%)
    pallas_call x1, Pallas kernels, local(): pl.pallas_call(functools.partial(layer_kernel, dims), in_specs=[vmem] * 3...  135 us
    unnamed x12, local copies, waits for them, and re-layouts  5.75 us

profile of v1, /device:TPU:0, one launch (start us, length us, event | category | flops | bytes accessed | tf_op | source)
XLA Modules:
  0.0 142.8 jit_solution(8767994873633676569)
XLA Ops:
  0.6 0.7 convert_element_type.3
  1.3 0.0 copy-start.3
  1.3 0.9 copy.11.col_ref
  2.2 0.0 copy-done.3
  2.2 134.9 %layer.1 = (bf16[512,1024]{1,0:T(8,128)(2,1)}, bf16[512,1024]{1,0:T(8,128)(2,1)}, bf16[512,1024]{1,0:T(8,128)(2,1)}, f32[512,1024]{1,0:T(8,128)}) custom-call(bf16[512,1024]{1,0:T(8,128)(2,1)} %q_ref.1, bf16[512,1024]{1,0:T(8,128)(2,1)} %k_ref.1, bf16[512,1024]{1,0:T(8,128)(2,1)} %v_ref.1, bf16[512,1024]{1,0:T(8,128)(2,1)} %go_hbm.1, ...), custom_call_target="tpu_custom_call" | custom-call | flops 12884901888 | bytes 25165824 | tf_op jit(solution)/shard_map/layer/pallas_call | solution.py:359
  137.0 0.0 copy-start.2
  137.1 0.0 copy-start.1
  137.1 2.4 %copy.16 = bf16[512,1024]{1,0:T(8,128)(2,1)} copy(bf16[512,1024]{1,0:T(8,128)(2,1)} %get-tuple-element.8) | data formatting | bytes 2097152
  139.5 0.0 copy-done.2
  139.5 0.0 copy-start
  139.5 1.0 copy.17
  140.4 0.0 copy-done.1
  140.4 1.0 copy.18
  141.4 0.1 copy-done
  141.5 1.3 copy.19
Async XLA Ops:
  1.3 0.9 copy-start.3
  137.0 2.4 %copy-start.2 = (bf16[512,1024]{1,0:T(8,128)(2,1)S(1)}, bf16[512,1024]{1,0:T(8,128)(2,1)}, u32[]{:S(2)}) copy-start(bf16[512,1024]{1,0:T(8,128)(2,1)} %get-tuple-element.9) | copy-start | bytes 3145732
  137.1 3.4 %copy-start.1 = (bf16[512,1024]{1,0:T(8,128)(2,1)S(1)}, bf16[512,1024]{1,0:T(8,128)(2,1)}, u32[]{:S(2)}) copy-start(bf16[512,1024]{1,0:T(8,128)(2,1)} %get-tuple-element.10) | copy-start | bytes 3145732
  139.5 2.0 %copy-start = (f32[512,1024]{1,0:T(8,128)S(1)}, f32[512,1024]{1,0:T(8,128)}, u32[]{:S(2)}) copy-start(f32[512,1024]{1,0:T(8,128)} %get-tuple-element.11) | copy-start | bytes 6291460

commit v2 on v1

--- a/solution.py
+++ b/solution.py
@@ -221,8 +221,8 @@
     def on_way(w, t):
         return (z <= t) if w == 0 else (z >= last - t)
 
-    def send_step(w, c, t):
-        @pl.when(on_way(w, t))
+    def send_step(w, c, t, when):
+        @pl.when(when)
         def _():
             dest = last - t + z if w == 0 else z - last + t
             acc[...] = partial(c, dest)
@@ -239,7 +239,7 @@
     for c in range(parts):
         pair_copy(c).wait_recv()
         for w in range(2):
-            send_step(w, c, 0)
+            send_step(w, c, 0, on_way(w, 0))
 
     load_w.wait()
     for c in range(chunks):
@@ -292,12 +292,15 @@
     def steps(t):
         for c in range(parts):
             for w in range(2):
-                send_step(w, c, t)
-
+                send_step(w, c, t, on_way(w, t) & (z > 0) if w == 0 else on_way(w, t))
+
+    for t in range(1, last):
+        for c in range(parts):
+            send_step(0, c, t, z == 0)
+    for c in range(chunks):
+        carry_on(1, c)
     for t in range(1, min(2, last)):
         steps(t)
-    for c in range(chunks):
-        carry_on(1, c)
     grads(0, heads // 2)
     for t in range(2, last):
         steps(t)

time: 143 us -> 135 us (0.944)
  the two profiles are of different devices: /device:TPU:0 before, /device:TPU:19 now
where the time goes in v2:
time: 135 us
  Pallas kernels  127 us (94%)
  local copies, waits for them, and re-layouts  6.61 us (5%)
    pallas_call x1, Pallas kernels, local(): pl.pallas_call(functools.partial(layer_kernel, dims), in_specs=[vmem] * 3...  127 us
    unnamed x12, local copies, waits for them, and re-layouts  5.75 us

profile of v2, /device:TPU:19, one launch (start us, length us, event | category | flops | bytes accessed | tf_op | source)
XLA Modules:
  0.0 134.6 jit_solution(4370043209801199378)
XLA Ops:
  0.6 0.7 convert_element_type.3
  1.3 0.0 copy-start.3
  1.3 0.9 copy.11.col_ref
  2.2 0.0 copy-done.3
  2.2 126.7 %layer.1 = (bf16[512,1024]{1,0:T(8,128)(2,1)}, bf16[512,1024]{1,0:T(8,128)(2,1)}, bf16[512,1024]{1,0:T(8,128)(2,1)}, f32[512,1024]{1,0:T(8,128)}) custom-call(bf16[512,1024]{1,0:T(8,128)(2,1)} %q_ref.1, bf16[512,1024]{1,0:T(8,128)(2,1)} %k_ref.1, bf16[512,1024]{1,0:T(8,128)(2,1)} %v_ref.1, bf16[512,1024]{1,0:T(8,128)(2,1)} %go_hbm.1, ...), custom_call_target="tpu_custom_call" | custom-call | flops 12884901888 | bytes 25165824 | tf_op jit(solution)/shard_map/layer/pallas_call | solution.py:362
  128.8 0.0 copy-start.2
  128.9 0.0 copy-start.1
  128.9 2.4 %copy.16 = bf16[512,1024]{1,0:T(8,128)(2,1)} copy(bf16[512,1024]{1,0:T(8,128)(2,1)} %get-tuple-element.8) | data formatting | bytes 2097152
  131.3 0.0 copy-done.2
  131.3 0.0 copy-start
  131.3 1.0 copy.17
  132.3 0.0 copy-done.1
  132.3 1.0 copy.18
  133.2 0.1 copy-done
  133.3 1.3 copy.19
Async XLA Ops:
  1.3 0.9 copy-start.3
  128.8 2.4 %copy-start.2 = (bf16[512,1024]{1,0:T(8,128)(2,1)S(1)}, bf16[512,1024]{1,0:T(8,128)(2,1)}, u32[]{:S(2)}) copy-start(bf16[512,1024]{1,0:T(8,128)(2,1)} %get-tuple-element.9) | copy-start | bytes 3145732
  128.9 3.4 %copy-start.1 = (bf16[512,1024]{1,0:T(8,128)(2,1)S(1)}, bf16[512,1024]{1,0:T(8,128)(2,1)}, u32[]{:S(2)}) copy-start(bf16[512,1024]{1,0:T(8,128)(2,1)} %get-tuple-element.10) | copy-start | bytes 3145732
  131.3 2.0 %copy-start = (f32[512,1024]{1,0:T(8,128)S(1)}, f32[512,1024]{1,0:T(8,128)}, u32[]{:S(2)}) copy-start(f32[512,1024]{1,0:T(8,128)} %get-tuple-element.11) | copy-start | bytes 6291460
